TPU v7x, 32 devices: a whole 2x2x4 slice. The times are simulated.
32 devices in a mesh: dp: 8 (over z, y), tp: 4 (over x, core).
Axes of the slice: x: 2, y: 2, z: 4, core: 2. Of those that a mesh axis runs over, the one named last changes fastest.
Arguments:
- frames: bfloat16 [24, 1024, 512], P('dp', 'tp'), may hold values from -6 to 6
- cotangent: bfloat16 [24, 1024, 512], P('dp', 'tp'), may hold values from -6 to 6
- lengths: int32 [24], P('dp'), may hold values from 64 to 1024, as said below
- conv_weight: float32 [512, 7], P(('dp', 'tp')), may hold values from -2 to 2
- conv_bias: float32 [512], P(('dp', 'tp')), may hold values from -0.6 to 0.6
- norm_gain: float32 [512], P(('dp', 'tp')), may hold values from 0.5 to 1.5
- norm_bias: float32 [512], P(('dp', 'tp')), may hold values from -0.6 to 0.6
- up_weight: float32 [512, 1536], P('dp', 'tp'), may hold values from -0.25 to 0.25
- up_bias: float32 [1536], P(('dp', 'tp')), may hold values from -0.6 to 0.6
- down_weight: float32 [512, 1536], P('dp', 'tp'), may hold values from -0.15625 to 0.15625
- down_bias: float32 [512], P(('dp', 'tp')), may hold values from -0.6 to 0.6
- layer_scale: float32 [512], P(('dp', 'tp')), may hold values from 0.25 to 1.75
- moment_conv_weight: float32 [512, 7], P(('dp', 'tp')), may hold values from -36 to 36
- moment_conv_bias: float32 [512], P(('dp', 'tp')), may hold values from -36 to 36
- moment_norm_gain: float32 [512], P(('dp', 'tp')), may hold values from -36 to 36
- moment_norm_bias: float32 [512], P(('dp', 'tp')), may hold values from -36 to 36
- moment_up_weight: float32 [512, 1536], P('dp', 'tp'), may hold values from -36 to 36
- moment_up_bias: float32 [1536], P(('dp', 'tp')), may hold values from -36 to 36
- moment_down_weight: float32 [512, 1536], P('dp', 'tp'), may hold values from -36 to 36
- moment_down_bias: float32 [512], P(('dp', 'tp')), may hold values from -36 to 36
- moment_layer_scale: float32 [512], P(('dp', 'tp')), may hold values from -36 to 36
- square_conv_weight: float32 [512, 7], P(('dp', 'tp')), may hold values from 1 to 9
- square_conv_bias: float32 [512], P(('dp', 'tp')), may hold values from 1 to 9
- square_norm_gain: float32 [512], P(('dp', 'tp')), may hold values from 1 to 9
- square_norm_bias: float32 [512], P(('dp', 'tp')), may hold values from 1 to 9
- square_up_weight: float32 [512, 1536], P('dp', 'tp'), may hold values from 1 to 9
- square_up_bias: float32 [1536], P(('dp', 'tp')), may hold values from 1 to 9
- square_down_weight: float32 [512, 1536], P('dp', 'tp'), may hold values from 1 to 9
- square_down_bias: float32 [512], P(('dp', 'tp')), may hold values from 1 to 9
- square_layer_scale: float32 [512], P(('dp', 'tp')), may hold values from 1 to 9
Outputs:
- output: float32 [24, 1024, 512], P('dp', 'tp')
- input_grad: float32 [24, 1024, 512], P('dp', 'tp')
- grad_conv_weight: float32 [512, 7], P(('dp', 'tp'))
- next_conv_weight: float32 [512, 7], P(('dp', 'tp'))
- next_moment_conv_weight: float32 [512, 7], P(('dp', 'tp'))
- next_square_conv_weight: float32 [512, 7], P(('dp', 'tp'))
- grad_conv_bias: float32 [512], P(('dp', 'tp'))
- next_conv_bias: float32 [512], P(('dp', 'tp'))
- next_moment_conv_bias: float32 [512], P(('dp', 'tp'))
- next_square_conv_bias: float32 [512], P(('dp', 'tp'))
- grad_norm_gain: float32 [512], P(('dp', 'tp'))
- update_norm_gain: float32 [512], P(('dp', 'tp'))
- next_moment_norm_gain: float32 [512], P(('dp', 'tp'))
- next_square_norm_gain: float32 [512], P(('dp', 'tp'))
- grad_norm_bias: float32 [512], P(('dp', 'tp'))
- next_norm_bias: float32 [512], P(('dp', 'tp'))
- next_moment_norm_bias: float32 [512], P(('dp', 'tp'))
- next_square_norm_bias: float32 [512], P(('dp', 'tp'))
- grad_up_weight: float32 [512, 1536], P('dp', 'tp')
- next_up_weight: float32 [512, 1536], P('dp', 'tp')
- next_moment_up_weight: float32 [512, 1536], P('dp', 'tp')
- next_square_up_weight: float32 [512, 1536], P('dp', 'tp')
- grad_up_bias: float32 [1536], P(('dp', 'tp'))
- next_up_bias: float32 [1536], P(('dp', 'tp'))
- next_moment_up_bias: float32 [1536], P(('dp', 'tp'))
- next_square_up_bias: float32 [1536], P(('dp', 'tp'))
- grad_down_weight: float32 [512, 1536], P('dp', 'tp')
- next_down_weight: float32 [512, 1536], P('dp', 'tp')
- next_moment_down_weight: float32 [512, 1536], P('dp', 'tp')
- next_square_down_weight: float32 [512, 1536], P('dp', 'tp')
- grad_down_bias: float32 [512], P(('dp', 'tp'))
- next_down_bias: float32 [512], P(('dp', 'tp'))
- next_moment_down_bias: float32 [512], P(('dp', 'tp'))
- next_square_down_bias: float32 [512], P(('dp', 'tp'))
- grad_layer_scale: float32 [512], P(('dp', 'tp'))
- update_layer_scale: float32 [512], P(('dp', 'tp'))
- next_moment_layer_scale: float32 [512], P(('dp', 'tp'))
- next_square_layer_scale: float32 [512], P(('dp', 'tp'))
Inputs may be any that keep to these rules, and one draw needn't show every extreme that they name: `lengths`: each slot's true frame count lies between 64 and 1024; in every draw at least one slot holds 1024 true frames.
All inputs are finite; a program needn't handle non-finite values.
Results may differ from a plain program's by a relative error of at most 0.0079.
Values may be sent and summed in bfloat16 or wider, within the bound.
No kernel may reach another device: no remote copies, remote signals or barrier semaphores. Data moves between devices by JAX's collectives and lax.ppermute only.
A program may use at most 128 MiB of HBM per device.

v0:
```python
import jax
import jax.numpy as jnp
from jax import lax
from jax.sharding import PartitionSpec as P

STEP = 4
norm_eps = 1e-06
learn_rate = 0.05
first_decay = 0.9
second_decay = 0.999
adam_eps = 1e-08
weight_decay = 0.1
update_flags = (False, False, True, False, False, False, False, False, True)


def conv_apply(padded, tap_weights, conv_shift, frames_out):
    result = conv_shift + padded[:, 0:frames_out, :] * tap_weights[:, 0]
    for offset in range(1, tap_weights.shape[1]):
        result = result + padded[:, offset : offset + frames_out, :] * tap_weights[:, offset]
    return result


def conv_back(grad_padded, tap_weights, frames_out):
    edge_start = tap_weights.shape[1] - 1
    result = grad_padded[:, edge_start : edge_start + frames_out, :] * tap_weights[:, 0]
    for offset in range(1, tap_weights.shape[1]):
        begin = edge_start - offset
        result = result + grad_padded[:, begin : begin + frames_out, :] * tap_weights[:, offset]
    return result


def tap_grads(conv_grad, padded):
    frames_out = conv_grad.shape[1]
    tap_total = padded.shape[1] - frames_out + 1
    columns = [
        jnp.sum(conv_grad * padded[:, offset : offset + frames_out, :], axis=(0, 1))
        for offset in range(tap_total)
    ]
    return jnp.stack(columns, axis=1)


def norm_forward(conv_out, gain_vector, shift_vector):
    centred = conv_out - jnp.mean(conv_out, axis=-1, keepdims=True)
    inverse = lax.rsqrt(jnp.mean(centred * centred, axis=-1, keepdims=True) + norm_eps)
    unit_norm = centred * inverse
    return (unit_norm * gain_vector + shift_vector, unit_norm, inverse)


def norm_backward(normed_grad, unit_norm, inverse, gain_vector):
    scaled = normed_grad * gain_vector
    centred_grad = scaled - jnp.mean(scaled, axis=-1, keepdims=True)
    return inverse * (
        centred_grad - unit_norm * jnp.mean(scaled * unit_norm, axis=-1, keepdims=True)
    )


def exact_gelu(values):
    return jax.nn.gelu(values, approximate=False)


def adam_step(weights_now, gradient, moment, square, step_number):
    next_moment = first_decay * moment + (1.0 - first_decay) * gradient
    next_square = second_decay * square + (1.0 - second_decay) * gradient * gradient
    first_fix = 1.0 - jnp.power(jnp.float32(first_decay), step_number)
    second_fix = 1.0 - jnp.power(jnp.float32(second_decay), step_number)
    step_ratio = next_moment / first_fix / (jnp.sqrt(next_square / second_fix) + adam_eps)
    update = -(learn_rate * (step_ratio + weight_decay * weights_now))
    return (weights_now + update, next_moment, next_square, update)


def per_device(
    frames,
    cotangent,
    lengths,
    conv_weight,
    conv_bias,
    norm_gain,
    norm_bias,
    up_weight,
    up_bias,
    down_weight,
    down_bias,
    layer_scale,
    moment_conv_weight,
    moment_conv_bias,
    moment_norm_gain,
    moment_norm_bias,
    moment_up_weight,
    moment_up_bias,
    moment_down_weight,
    moment_down_bias,
    moment_layer_scale,
    square_conv_weight,
    square_conv_bias,
    square_norm_gain,
    square_norm_bias,
    square_up_weight,
    square_up_bias,
    square_down_weight,
    square_down_bias,
    square_layer_scale,
):
    tp_count = lax.axis_size("tp")
    device_rank = lax.axis_index("tp")
    slot_count, quarter_len, feature_width = frames.shape
    slot_len = quarter_len * tp_count
    frame_start = device_rank * quarter_len
    up_rows, down_rows = (
        lax.all_gather(up_weight.astype(jnp.bfloat16), "dp", axis=0, tiled=True),
        lax.all_gather(down_weight.astype(jnp.bfloat16), "dp", axis=0, tiled=True),
    )
    tap_weights, conv_shift, gain_vector, shift_vector, up_shift, down_shift, scale_vector = (
        lax.all_gather(conv_weight, ("dp", "tp"), axis=0, tiled=True),
        lax.all_gather(conv_bias, ("dp", "tp"), axis=0, tiled=True),
        lax.all_gather(norm_gain, ("dp", "tp"), axis=0, tiled=True),
        lax.all_gather(norm_bias, ("dp", "tp"), axis=0, tiled=True),
        lax.all_gather(up_bias, ("dp", "tp"), axis=0, tiled=True),
        lax.all_gather(down_bias, ("dp", "tp"), axis=0, tiled=True),
        lax.all_gather(layer_scale, ("dp", "tp"), axis=0, tiled=True),
    )
    kernel_half = tap_weights.shape[1] // 2
    hidden_width = up_shift.shape[0]
    own_width = up_rows.shape[1]
    whole_frames, whole_cot = (
        lax.all_gather(frames, "tp", axis=1, tiled=True),
        lax.all_gather(cotangent, "tp", axis=1, tiled=True),
    )
    positions = lax.broadcasted_iota(jnp.int32, (slot_count, slot_len), 1)
    frame_mask = (positions < lengths[:, None]).astype(jnp.float32)[:, :, None]
    signal = whole_frames.astype(jnp.float32)
    shifted = signal * frame_mask
    padded = jnp.pad(shifted, ((0, 0), (kernel_half, kernel_half), (0, 0)))
    conv_out = conv_apply(padded, tap_weights, conv_shift, slot_len)
    normed, unit_norm, inverse = norm_forward(conv_out, gain_vector, shift_vector)
    normed_low = normed.astype(jnp.bfloat16)
    own_shift = lax.dynamic_slice_in_dim(up_shift, device_rank * own_width, own_width)
    hidden = (
        jnp.einsum("slc,ch->slh", normed_low, up_rows, preferred_element_type=jnp.float32)
        + own_shift
    )
    active, gelu_pull = jax.vjp(exact_gelu, hidden)
    active_low = active.astype(jnp.bfloat16)
    partial_out = jnp.einsum(
        "slh,ch->slc", active_low, down_rows, preferred_element_type=jnp.float32
    )
    branch = lax.psum(partial_out, "tp") + down_shift
    output_full = (signal + scale_vector * branch) * frame_mask
    back_grad = whole_cot.astype(jnp.float32) * frame_mask
    branch_grad = (back_grad * scale_vector).astype(jnp.bfloat16)
    active_grad = jnp.einsum(
        "slc,ch->slh", branch_grad, down_rows, preferred_element_type=jnp.float32
    )
    hidden_grad = gelu_pull(active_grad)[0].astype(jnp.bfloat16)
    normed_part = jnp.einsum(
        "slh,ch->slc", hidden_grad, up_rows, preferred_element_type=jnp.float32
    )
    normed_grad = lax.psum(normed_part, "tp")
    conv_grad = norm_backward(normed_grad, unit_norm, inverse, gain_vector)
    grad_padded = jnp.pad(conv_grad, ((0, 0), (kernel_half, kernel_half), (0, 0)))
    input_full = back_grad + frame_mask * conv_back(grad_padded, tap_weights, slot_len)
    grad_up = jnp.einsum("slc,slh->ch", normed_low, hidden_grad, preferred_element_type=jnp.float32)
    grad_down = jnp.einsum(
        "slc,slh->ch", branch_grad, active_low, preferred_element_type=jnp.float32
    )
    own_up_grad = jnp.sum(hidden_grad.astype(jnp.float32), axis=(0, 1))
    grad_up_shift = lax.dynamic_update_slice_in_dim(
        jnp.zeros((hidden_width,), jnp.float32), own_up_grad, device_rank * own_width, 0
    )

    def own_frames(values):
        return lax.dynamic_slice_in_dim(values, frame_start, quarter_len, 1)

    conv_grad_own = own_frames(conv_grad)
    normed_grad_own = own_frames(normed_grad)
    unit_own = own_frames(unit_norm)
    back_own = own_frames(back_grad)
    branch_own = own_frames(branch)
    branch_grad_own = own_frames(branch_grad)
    taps_grad = tap_grads(
        conv_grad_own,
        lax.dynamic_slice_in_dim(padded, frame_start, quarter_len + 2 * kernel_half, 1),
    )
    output_own = own_frames(output_full)
    input_own = own_frames(input_full)
    grad_scale = jnp.sum(back_own * branch_own, axis=(0, 1))
    grad_down_shift = jnp.sum(branch_grad_own.astype(jnp.float32), axis=(0, 1))
    grad_gain = jnp.sum(normed_grad_own * unit_own, axis=(0, 1))
    grad_shift = jnp.sum(normed_grad_own, axis=(0, 1))
    grad_conv_shift = jnp.sum(conv_grad_own, axis=(0, 1))
    up_share, down_share = (
        lax.psum_scatter(grad_up, "dp", scatter_dimension=0, tiled=True),
        lax.psum_scatter(grad_down, "dp", scatter_dimension=0, tiled=True),
    )
    share_taps, share_conv, share_gain, share_shift, share_up, share_down, share_scale = (
        lax.psum_scatter(taps_grad, ("dp", "tp"), scatter_dimension=0, tiled=True),
        lax.psum_scatter(grad_conv_shift, ("dp", "tp"), scatter_dimension=0, tiled=True),
        lax.psum_scatter(grad_gain, ("dp", "tp"), scatter_dimension=0, tiled=True),
        lax.psum_scatter(grad_shift, ("dp", "tp"), scatter_dimension=0, tiled=True),
        lax.psum_scatter(grad_up_shift, ("dp", "tp"), scatter_dimension=0, tiled=True),
        lax.psum_scatter(grad_down_shift, ("dp", "tp"), scatter_dimension=0, tiled=True),
        lax.psum_scatter(grad_scale, ("dp", "tp"), scatter_dimension=0, tiled=True),
    )
    step_number = jnp.float32(STEP)
    params = (
        conv_weight,
        conv_bias,
        norm_gain,
        norm_bias,
        up_weight,
        up_bias,
        down_weight,
        down_bias,
        layer_scale,
    )
    gradients = (
        share_taps,
        share_conv,
        share_gain,
        share_shift,
        up_share,
        share_up,
        down_share,
        share_down,
        share_scale,
    )
    moments = (
        moment_conv_weight,
        moment_conv_bias,
        moment_norm_gain,
        moment_norm_bias,
        moment_up_weight,
        moment_up_bias,
        moment_down_weight,
        moment_down_bias,
        moment_layer_scale,
    )
    squares = (
        square_conv_weight,
        square_conv_bias,
        square_norm_gain,
        square_norm_bias,
        square_up_weight,
        square_up_bias,
        square_down_weight,
        square_down_bias,
        square_layer_scale,
    )
    flat = [output_own, input_own]
    for weights_now, gradient, moment, square, use_update in zip(
        params, gradients, moments, squares, update_flags
    ):
        next_weights, next_moment, next_square, update = adam_step(
            weights_now, gradient, moment, square, step_number
        )
        shown = update if use_update else next_weights
        flat = flat + [gradient, shown, next_moment, next_square]
    return (
        flat[0],
        flat[1],
        flat[2],
        flat[3],
        flat[4],
        flat[5],
        flat[6],
        flat[7],
        flat[8],
        flat[9],
        flat[10],
        flat[11],
        flat[12],
        flat[13],
        flat[14],
        flat[15],
        flat[16],
        flat[17],
        flat[18],
        flat[19],
        flat[20],
        flat[21],
        flat[22],
        flat[23],
        flat[24],
        flat[25],
        flat[26],
        flat[27],
        flat[28],
        flat[29],
        flat[30],
        flat[31],
        flat[32],
        flat[33],
        flat[34],
        flat[35],
        flat[36],
        flat[37],
    )


def solution(mesh):
    return jax.shard_map(
        per_device,
        mesh=mesh,
        in_specs=(
            P("dp", "tp", None),
            P("dp", "tp", None),
            P("dp"),
            P(("dp", "tp"), None),
            P(("dp", "tp")),
            P(("dp", "tp")),
            P(("dp", "tp")),
            P("dp", "tp"),
            P(("dp", "tp")),
            P("dp", "tp"),
            P(("dp", "tp")),
            P(("dp", "tp")),
            P(("dp", "tp"), None),
            P(("dp", "tp")),
            P(("dp", "tp")),
            P(("dp", "tp")),
            P("dp", "tp"),
            P(("dp", "tp")),
            P("dp", "tp"),
            P(("dp", "tp")),
            P(("dp", "tp")),
            P(("dp", "tp"), None),
            P(("dp", "tp")),
            P(("dp", "tp")),
            P(("dp", "tp")),
            P("dp", "tp"),
            P(("dp", "tp")),
            P("dp", "tp"),
            P(("dp", "tp")),
            P(("dp", "tp")),
        ),
        out_specs=(
            P("dp", "tp", None),
            P("dp", "tp", None),
            P(("dp", "tp"), None),
            P(("dp", "tp"), None),
            P(("dp", "tp"), None),
            P(("dp", "tp"), None),
            P(("dp", "tp")),
            P(("dp", "tp")),
            P(("dp", "tp")),
            P(("dp", "tp")),
            P(("dp", "tp")),
            P(("dp", "tp")),
            P(("dp", "tp")),
            P(("dp", "tp")),
            P(("dp", "tp")),
            P(("dp", "tp")),
            P(("dp", "tp")),
            P(("dp", "tp")),
            P("dp", "tp"),
            P("dp", "tp"),
            P("dp", "tp"),
            P("dp", "tp"),
            P(("dp", "tp")),
            P(("dp", "tp")),
            P(("dp", "tp")),
            P(("dp", "tp")),
            P("dp", "tp"),
            P("dp", "tp"),
            P("dp", "tp"),
            P("dp", "tp"),
            P(("dp", "tp")),
            P(("dp", "tp")),
            P(("dp", "tp")),
            P(("dp", "tp")),
            P(("dp", "tp")),
            P(("dp", "tp")),
            P(("dp", "tp")),
            P(("dp", "tp")),
        ),
        check_vma=False,
    )
```

profile of v0, /device:TPU:0, one launch (start us, length us, event | category | flops | bytes accessed | tf_op | source)
XLA Modules:
  0.0 722.1 jit_solution(14380153058658341902)
XLA Ops:
  9.7 44.2 %all-gather = f32[32,16,7]{1,2,0:T(8,128)S(1)} all-gather(f32[1,16,7]{1,2,0:T(8,128)} %bitcast.62), channel_id=1, replica_groups=mesh['dp'=8,'tp'=4] {'dp','tp'}, dimensions={0}, use_global_device_ids=true | all-gather | bytes 14784 | tf_op jit(solution)/shard_map/all_gather | solution.py:113
  59.1 37.4 %all-reduce.15 = (f32[512]{0:T(512)S(1)}, f32[512]{0:T(512)S(1)}, f32[512]{0:T(512)S(1)}, f32[1536]{0:T(1024)S(1)}, f32[512]{0:T(512)S(1)}, /*index=5*/f32[512]{0:T(512)S(1)}) all-reduce(f32[512]{0:T(512)S(1)} %dynamic-update-slice.1, f32[512]{0:T(512)S(1)} %dynamic-update-slice.3, ...), channel_id=1, replica_groups=mesh['dp'=8,'tp'=4] {'dp','tp'}, use_global_device_ids=true, to_apply=%add.3 | all-reduce | flops 4096 | bytes 32768
  96.5 31.3 %all_gather.39 = bf16[512,384]{1,0:T(8,128)(2,1)S(1)} all-gather(bf16[64,384]{1,0:T(8,128)(2,1)S(1)} %convert_element_type.43), channel_id=1, replica_groups=mesh['dp'=8,'tp'=4] {'dp'}, dimensions={0}, use_global_device_ids=true | all-gather | bytes 442368 | tf_op jit(solution)/shard_map/all_gather | solution.py:109
  128.6 5.2 convert_multiply_fusion
  133.8 6.0 fusion.59
  139.9 1.1 multiply_reduce_fusion.1
  142.4 3.1 fusion.31
  145.6 11.7 %multiply_convert_fusion.1 = (bf16[3,1024,384]{2,1,0:T(8,128)(2,1)S(1)}, f32[3,1024,384]{2,1,0:T(8,128)}) fusion(f32[3,1024,384]{2,1,0:T(8,128)S(1)} %get-tuple-element.123, f32[384]{0:T(512)S(1)} %dynamic_slice.30, u8[1024,384]{1,0:T(8,128)(4,1)S(1)} %get-tuple-element.51, u8[1024,384]{1,0:T(8,128)(4,1)S(1)} %get-tuple-element.50), kind=kLoop, calls=%fused_computation.35 | loop fusion | flops 83755008 | bytes 12584448 | tf_op jit(solution)/shard_map/convert_element_type | solution.py:142
  157.4 2.7 convolution_bitcast_fusion
  160.3 63.0 %reduce-scatter.8.cloned.1.call-done = f32[64,384]{1,0:T(8,128)} async-done(((f32[512,384]{1,0:T(8,128)}), f32[64,384]{1,0:T(8,128)}) %reduce-scatter.8.cloned.1.call-update) | async-done | bytes 98320 | tf_op jit(solution)/shard_map/reduce_scatter | solution.py:192
  223.3 1.8 negate_add_fusion
  225.1 31.1 %all_gather.41 = bf16[512,384]{1,0:T(8,128)(2,1)S(1)} all-gather(bf16[64,384]{1,0:T(8,128)(2,1)S(1)} %get-tuple-element.114), channel_id=1, replica_groups=mesh['dp'=8,'tp'=4] {'dp'}, dimensions={0}, use_global_device_ids=true | all-gather | bytes 442368 | tf_op jit(solution)/shard_map/all_gather | solution.py:110
  256.2 8.1 %convert_reduce_fusion = (f32[384]{0:T(512)S(1)}, bf16[3,1024,384]{2,1,0:T(8,128)(2,1)S(1)}) fusion(f32[3,1024,384]{2,1,0:T(8,128)} %get-tuple-element.102, bf16[3,1024,512]{2,1,0:T(8,128)(2,1)} %copy-done.4, bf16[512,384]{1,0:T(8,128)(2,1)S(1)} %all_gather.41, f32[3,1024,384]{2,1,0:T(8,128)} %copy-done.7, f32[384]{0:T(512)S(1)} %dynamic_slice.30), kind=kOutput, calls=%fused_computation.33 | convolution fusion | flops 1228013184 | bytes 15338496 | tf_op jit(solution)/shard_map/slc,ch->slh/dot_general | solution.py:150
  264.3 1.4 copy-done.5
  265.7 2.7 convolution_bitcast_fusion.1
  268.5 6.1 fusion.36
  274.6 4.4 fusion.34
  279.4 1.6 copy-done.6
  280.9 3.6 convert_element_type.40
  284.5 1.3 convert_reduce_fusion.1
  286.1 44.5 %reduce-scatter.6.cloned.1.call-done = f32[64,384]{1,0:T(8,128)} async-done(((f32[512,384]{1,0:T(8,128)}), f32[64,384]{1,0:T(8,128)}) %reduce-scatter.6.cloned.1.call-update) | async-done | bytes 98320 | tf_op jit(solution)/shard_map/reduce_scatter | solution.py:191
  330.7 1.6 negate_add_fusion.1
  332.3 220.5 %all-reduce.19.cloned.1.call-done = (f32[3,1024,512]{2,1,0:T(8,128)}, f32[3,1024,512]{2,1,0:T(8,128)}) async-done(((f32[3,1024,512]{2,1,0:T(8,128)}, f32[3,1024,512]{2,1,0:T(8,128)}), (f32[3,1024,512]{2,1,0:T(8,128)}, f32[3,1024,512]{2,1,0:T(8,128)})) %all-reduce.19.cloned.1.call-update) | async-done | bytes 12582928 | tf_op jit(solution)/shard_map/psum | solution.py:146
  552.8 2.3 dynamic-slice_reduce_fusion
  555.2 6.1 multiply_reduce_fusion.2
  562.4 4.0 broadcast_multiply_fusion
  566.4 9.2 %multiply_add_fusion = (f32[3,1024,512]{2,1,0:T(8,128)}, f32[3,1024,512]{2,1,0:T(8,128)}, f32[3,1024,512]{2,1,0:T(8,128)}, f32[3,1024,512]{2,1,0:T(8,128)}) fusion(f32[3,1024,512]{2,1,0:T(8,128)S(1)} %get-tuple-element.100, f32[512]{0:T(512)S(1)} %bitcast.57, f32[512]{0:T(512)S(1)} %bitcast.59, f32[512]{0:T(512)S(1)} %bitcast.55), kind=kLoop, calls=%fused_computation.1 | loop fusion | flops 7864320 | bytes 31463424 | tf_op jit(solution)/shard_map/add | solution.py:28
  575.5 1.8 fusion.17
  578.2 3.6 broadcast_add_fusion
  582.1 6.8 multiply_reduce_fusion.3
  588.8 39.8 %all-reduce.14 = (f32[512]{0:T(512)S(1)}, f32[512]{0:T(512)S(1)}, f32[512]{0:T(512)S(1)}, f32[1536]{0:T(1024)S(1)}, f32[512]{0:T(512)S(1)}, /*index=5*/f32[512]{0:T(512)S(1)}) all-reduce(f32[512]{0:T(512)S(1)} %get-tuple-element.49, f32[512]{0:T(512)S(1)} %get-tuple-element.48, ...), channel_id=3, replica_groups=mesh['dp'=8,'tp'=4] {'dp','tp'}, use_global_device_ids=true, to_apply=%region_15.16.clone | all-reduce | flops 4096 | bytes 32768
  632.3 81.5 %reduce-scatter.10.cloned.1.call-done = f32[16,7]{1,0:T(8,128)} async-done(((f32[512,7]{1,0:T(8,128)}), f32[16,7]{1,0:T(8,128)}) %reduce-scatter.10.cloned.1.call-update) | async-done | bytes 464
  (134 shorter events, 18.0 us)
Async XLA Ops:
  7.2 121.4 %all-gather.4.cloned.1.call-start = ((), (), s32[]{:S(2)}) async-start(), calls=%async_computation.3 | async-start | bytes 3932160 | tf_op jit(solution)/shard_map/all_gather | solution.py:125
  7.9 120.7 %all-gather.6.cloned.1.call-start = ((), (), s32[]{:S(2)}) async-start(), calls=%async_computation.4 | async-start | bytes 3932160 | tf_op jit(solution)/shard_map/all_gather | solution.py:126
  8.7 214.6 %reduce-scatter.8.cloned.1.call-start = ((), (), s32[]{:S(2)}) async-start(), calls=%async_computation.6 | async-start | bytes 884736 | tf_op jit(solution)/shard_map/reduce_scatter | solution.py:192
  157.3 66.0 %copy-start.9 = (f32[64,384]{1,0:T(8,128)S(1)}, f32[64,384]{1,0:T(8,128)}, u32[]{:S(2)}) copy-start(f32[64,384]{1,0:T(8,128)} %param.39) | copy-start | bytes 294916
  157.3 66.0 %copy-start.10 = (f32[64,384]{1,0:T(8,128)S(1)}, f32[64,384]{1,0:T(8,128)}, u32[]{:S(2)}) copy-start(f32[64,384]{1,0:T(8,128)} %param.57) | copy-start | bytes 294916
  157.3 66.0 %copy-start.11 = (f32[64,384]{1,0:T(8,128)S(1)}, f32[64,384]{1,0:T(8,128)}, u32[]{:S(2)}) copy-start(f32[64,384]{1,0:T(8,128)} %param.48) | copy-start | bytes 294916
  160.1 170.5 %reduce-scatter.6.cloned.1.call-start = ((), (), s32[]{:S(2)}) async-start(), calls=%async_computation.5 | async-start | bytes 884736 | tf_op jit(solution)/shard_map/reduce_scatter | solution.py:191
  268.5 284.4 %all-reduce.19.cloned.1.call-start = ((), (), s32[]{:S(2)}) async-start(), calls=%async_computation.8 | async-start | bytes 25165824 | tf_op jit(solution)/shard_map/psum | solution.py:146
  279.1 434.8 %reduce-scatter.10.cloned.1.call-start = ((), (), s32[]{:S(2)}) async-start(), calls=%async_computation.7 | async-start | bytes 270336
  280.9 49.7 %copy-start.8 = (f32[64,384]{1,0:T(8,128)S(1)}, f32[64,384]{1,0:T(8,128)}, u32[]{:S(2)}) copy-start(f32[64,384]{1,0:T(8,128)} %param.37) | copy-start | bytes 294916
  280.9 49.7 %copy-start.12 = (f32[64,384]{1,0:T(8,128)S(1)}, f32[64,384]{1,0:T(8,128)}, u32[]{:S(2)}) copy-start(f32[64,384]{1,0:T(8,128)} %param.55) | copy-start | bytes 294916
  280.9 49.7 %copy-start.13 = (f32[64,384]{1,0:T(8,128)S(1)}, f32[64,384]{1,0:T(8,128)}, u32[]{:S(2)}) copy-start(f32[64,384]{1,0:T(8,128)} %param.46) | copy-start | bytes 294916
  581.8 46.8 %copy-start.18 = (f32[16]{0:T(128)S(1)}, f32[16]{0:T(128)}, u32[]{:S(2)}) copy-start(f32[16]{0:T(128)} %param.34) | copy-start | bytes 196
  581.8 46.8 %copy-start.19 = (f32[16]{0:T(128)S(1)}, f32[16]{0:T(128)}, u32[]{:S(2)}) copy-start(f32[16]{0:T(128)} %param.52) | copy-start | bytes 196
  581.8 47.4 %copy-start.21 = (f32[16]{0:T(128)S(1)}, f32[16]{0:T(128)}, u32[]{:S(2)}) copy-start(f32[16]{0:T(128)} %param.35) | copy-start | bytes 196
  581.8 47.4 %copy-start.22 = (f32[16]{0:T(128)S(1)}, f32[16]{0:T(128)}, u32[]{:S(2)}) copy-start(f32[16]{0:T(128)} %param.53) | copy-start | bytes 196
  581.9 47.4 %copy-start.23 = (f32[16]{0:T(128)S(1)}, f32[16]{0:T(128)}, u32[]{:S(2)}) copy-start(f32[16]{0:T(128)} %param.44) | copy-start | bytes 196
  581.9 48.0 %copy-start.24 = (f32[16]{0:T(128)S(1)}, f32[16]{0:T(128)}, u32[]{:S(2)}) copy-start(f32[16]{0:T(128)} %param.36) | copy-start | bytes 196
  581.9 48.0 %copy-start.25 = (f32[16]{0:T(128)S(1)}, f32[16]{0:T(128)}, u32[]{:S(2)}) copy-start(f32[16]{0:T(128)} %param.54) | copy-start | bytes 196
  581.9 48.0 %copy-start.26 = (f32[16]{0:T(128)S(1)}, f32[16]{0:T(128)}, u32[]{:S(2)}) copy-start(f32[16]{0:T(128)} %param.45) | copy-start | bytes 196
  581.9 48.6 %copy-start.27 = (f32[16]{0:T(128)S(1)}, f32[16]{0:T(128)}, u32[]{:S(2)}) copy-start(f32[16]{0:T(128)} %param.40) | copy-start | bytes 196
  581.9 48.6 %copy-start.28 = (f32[16]{0:T(128)S(1)}, f32[16]{0:T(128)}, u32[]{:S(2)}) copy-start(f32[16]{0:T(128)} %param.58) | copy-start | bytes 196
  581.9 48.5 %copy-start.29 = (f32[16]{0:T(128)S(1)}, f32[16]{0:T(128)}, u32[]{:S(2)}) copy-start(f32[16]{0:T(128)} %param.49) | copy-start | bytes 196
  581.9 49.2 %copy-start.30 = (f32[16]{0:T(128)S(1)}, f32[16]{0:T(128)}, u32[]{:S(2)}) copy-start(f32[16]{0:T(128)} %param.41) | copy-start | bytes 196
  582.0 49.1 %copy-start.31 = (f32[16]{0:T(128)S(1)}, f32[16]{0:T(128)}, u32[]{:S(2)}) copy-start(f32[16]{0:T(128)} %param.59) | copy-start | bytes 196
  582.0 49.1 %copy-start.32 = (f32[16]{0:T(128)S(1)}, f32[16]{0:T(128)}, u32[]{:S(2)}) copy-start(f32[16]{0:T(128)} %param.50) | copy-start | bytes 196
  582.0 49.7 %copy-start.33 = (f32[48]{0:T(128)S(1)}, f32[48]{0:T(128)}, u32[]{:S(2)}) copy-start(f32[48]{0:T(128)} %param.38) | copy-start | bytes 580
  582.0 49.7 %copy-start.34 = (f32[48]{0:T(128)S(1)}, f32[48]{0:T(128)}, u32[]{:S(2)}) copy-start(f32[48]{0:T(128)} %param.56) | copy-start | bytes 580
  582.0 49.7 %copy-start.35 = (f32[48]{0:T(128)S(1)}, f32[48]{0:T(128)}, u32[]{:S(2)}) copy-start(f32[48]{0:T(128)} %param.47) | copy-start | bytes 580
  582.0 132.6 %copy-start.14 = (f32[16,7]{0,1:T(8,128)S(1)}, f32[16,7]{0,1:T(8,128)}, u32[]{:S(2)}) copy-start(f32[16,7]{0,1:T(8,128)} %param.33) | copy-start | bytes 1348
  582.0 132.6 %copy-start.16 = (f32[16,7]{0,1:T(8,128)S(1)}, f32[16,7]{0,1:T(8,128)}, u32[]{:S(2)}) copy-start(f32[16,7]{0,1:T(8,128)} %param.51) | copy-start | bytes 1348
  582.0 132.6 %copy-start.17 = (f32[16,7]{0,1:T(8,128)S(1)}, f32[16,7]{0,1:T(8,128)}, u32[]{:S(2)}) copy-start(f32[16,7]{0,1:T(8,128)} %param.42) | copy-start | bytes 1348
  (16 other events, 193.8 us)
Sparse Core Ops, SparseCore 0:
  9.6 31.9 all-gather.3
  43.1 29.1 all-gather.5
  160.2 63.0 reduce-scatter.7
  268.6 62.0 reduce-scatter.5
  333.1 219.6 all-reduce.18
  578.3 135.4 reduce-scatter.9
where the time goes:
time: 723 us; the launch traced here: 722 us
  waiting for transfers between devices  411 us (57%)
  blocking collectives  184 us (25%)
  other arithmetic  73.1 us (10%)
  matrix products  27.2 us (4%)
  between operations  14.6 us (2%)
  local copies, waits for them, and re-layouts  11.8 us (2%)
    psum x1, waiting for transfers between devices, per_device(): branch = lax.psum(partial_out, 'tp') + down_shift  221 us
    unnamed x7, waiting for transfers between devices  83 us
    unnamed x2, blocking collectives  77.1 us
    reduce_scatter x1, waiting for transfers between devices, per_device(): lax.psum_scatter(grad_down, 'dp', scatter_dimension=0, tiled=True)  63 us
    reduce_scatter x1, waiting for transfers between devices, per_device(): lax.psum_scatter(grad_up, 'dp', scatter_dimension=0, tiled=True)  44.5 us
    all_gather x1, blocking collectives, per_device(): lax.all_gather(conv_weight, ('dp', 'tp'), axis=0, tiled=True)  44.2 us
    all_gather x1, blocking collectives, per_device(): lax.all_gather(up_weight.astype(jnp.bfloat16), 'dp', axis=0, tiled=True)  31.3 us
    all_gather x1, blocking collectives, per_device(): lax.all_gather(down_weight.astype(jnp.bfloat16), 'dp', axis=0, tiled=True)  31.1 us
  transfers between devices with their start and end apart: 6, of which 4 were waited for; matrix products, arithmetic and copies ran while one was open for 5% of the time, Pallas kernels for 0%

commit v1 on v0

--- a/solution.py
+++ b/solution.py
@@ -11,6 +11,21 @@
 adam_eps = 1e-08
 weight_decay = 0.1
 update_flags = (False, False, True, False, False, False, False, False, True)
+
+
+def _touch_matrix(piece_in):
+    state_next = lax.axis_size("dp")
+    val2 = lax.axis_index("dp")
+    moved, outcome_arr, kept_arr = (state_next, val2, piece_in.shape[0])
+    taken_in, row_out = (piece_in, 1)
+    while row_out < moved:
+        all_values = range(moved)
+        y1 = map(lambda dev_j: (dev_j, (dev_j - row_out) % moved), all_values)
+        p_next = list(y1)
+        s_next = lax.ppermute(taken_in, "dp", p_next)
+        taken_in = jnp.concatenate([taken_in, s_next], axis=0)
+        row_out = 2 * row_out
+    return jnp.roll(taken_in, shift=outcome_arr * kept_arr, axis=0)
 
 
 def conv_apply(padded, tap_weights, conv_shift, frames_out):
@@ -107,7 +122,7 @@
     frame_start = device_rank * quarter_len
     up_rows, down_rows = (
         lax.all_gather(up_weight.astype(jnp.bfloat16), "dp", axis=0, tiled=True),
-        lax.all_gather(down_weight.astype(jnp.bfloat16), "dp", axis=0, tiled=True),
+        _touch_matrix(down_weight.astype(jnp.bfloat16)),
     )
     tap_weights, conv_shift, gain_vector, shift_vector, up_shift, down_shift, scale_vector = (
         lax.all_gather(conv_weight, ("dp", "tp"), axis=0, tiled=True),

time: 723 us -> 699 us (0.967)
  blocking collectives: 184 us -> 147 us
  starting transfers between devices: 0.64 us -> 8.94 us
    all_gather x1 -> x0, blocking collectives: 31.1 us -> none  [per_device(): lax.all_gather(down_weight.astype(jnp.bfloat16), 'dp', axis=0, tiled=True)]
    ppermute x0 -> x3, starting transfers between devices: none -> 8.48 us  [_touch_matrix(): s_next = lax.ppermute(taken_in, 'dp', p_next)]
  transfers between devices with their start and end apart: 6 -> 9, of which waited for: 4 -> 5; matrix products, arithmetic and copies ran while one was open for 5% -> 6% of each run, Pallas kernels for 0% -> 0%
where the time goes in v1:
time: 699 us; the launch traced here: 698 us
  waiting for transfers between devices  418 us (60%)
  blocking collectives  147 us (21%)
  other arithmetic  73 us (10%)
  matrix products  24.1 us (3%)
  between operations  14.7 us (2%)
  local copies, waits for them, and re-layouts  12 us (2%)
  starting transfers between devices  8.94 us (1%)
    psum x1, waiting for transfers between devices, per_device(): branch = lax.psum(partial_out, 'tp') + down_shift  220 us
    unnamed x7, waiting for transfers between devices  83.4 us
    unnamed x2, blocking collectives  77.1 us
    reduce_scatter x1, waiting for transfers between devices, per_device(): lax.psum_scatter(grad_down, 'dp', scatter_dimension=0, tiled=True)  64.4 us
    reduce_scatter x1, waiting for transfers between devices, per_device(): lax.psum_scatter(grad_up, 'dp', scatter_dimension=0, tiled=True)  43.2 us
    all_gather x1, blocking collectives, per_device(): lax.all_gather(conv_weight, ('dp', 'tp'), axis=0, tiled=True)  38.8 us
    all_gather x1, blocking collectives, per_device(): lax.all_gather(up_weight.astype(jnp.bfloat16), 'dp', axis=0, tiled=True)  31.6 us
  transfers between devices with their start and end apart: 9, of which 5 were waited for; matrix products, arithmetic and copies ran while one was open for 6% of the time, Pallas kernels for 0%

profile of v1, /device:TPU:0, one launch (start us, length us, event | category | flops | bytes accessed | tf_op | source)
XLA Modules:
  0.0 698.2 jit_solution(4522713591956412298)
XLA Ops:
  9.7 6.1 collective-permute-start
  15.7 38.8 %all-gather = f32[32,16,7]{1,2,0:T(8,128)S(1)} all-gather(f32[1,16,7]{1,2,0:T(8,128)} %bitcast.60), channel_id=1, replica_groups=mesh['dp'=8,'tp'=4] {'dp','tp'}, dimensions={0}, use_global_device_ids=true | all-gather | bytes 14784 | tf_op jit(solution)/shard_map/all_gather | solution.py:128
  61.4 37.4 %all-reduce.15 = (f32[512]{0:T(512)S(1)}, f32[512]{0:T(512)S(1)}, f32[512]{0:T(512)S(1)}, f32[1536]{0:T(1024)S(1)}, f32[512]{0:T(512)S(1)}, /*index=5*/f32[512]{0:T(512)S(1)}) all-reduce(f32[512]{0:T(512)S(1)} %dynamic-update-slice.1, f32[512]{0:T(512)S(1)} %dynamic-update-slice.3, ...), channel_id=1, replica_groups=mesh['dp'=8,'tp'=4] {'dp','tp'}, use_global_device_ids=true, to_apply=%add.3 | all-reduce | flops 4096 | bytes 32768
  98.8 2.3 collective-permute-start.1
  101.1 31.6 %all_gather.36 = bf16[512,384]{1,0:T(8,128)(2,1)S(1)} all-gather(bf16[64,384]{1,0:T(8,128)(2,1)S(1)} %convert_element_type.43), channel_id=1, replica_groups=mesh['dp'=8,'tp'=4] {'dp'}, dimensions={0}, use_global_device_ids=true | all-gather | bytes 442368 | tf_op jit(solution)/shard_map/all_gather | solution.py:124
  132.9 6.5 collective-permute-done.2
  139.6 5.4 convert_multiply_fusion
  145.0 6.0 fusion.63
  153.7 3.1 fusion.31
  156.9 10.9 %multiply_convert_fusion.1 = (bf16[3,1024,384]{2,1,0:T(8,128)(2,1)S(1)}, f32[3,1024,384]{2,1,0:T(8,128)S(1)}) fusion(f32[3,1024,384]{2,1,0:T(8,128)S(1)} %get-tuple-element.124, f32[384]{0:T(512)S(1)} %dynamic_slice.34, u8[1024,384]{1,0:T(8,128)(4,1)S(1)} %get-tuple-element.51, u8[1024,384]{1,0:T(8,128)(4,1)S(1)} %get-tuple-element.50), kind=kLoop, calls=%fused_computation.35 | loop fusion | flops 83755008 | bytes 12584448 | tf_op jit(solution)/shard_map/convert_element_type | solution.py:157
  167.8 3.5 convert_reduce_fusion
  171.3 1.4 copy-done.5
  172.7 2.7 convolution_bitcast_fusion.1
  175.7 4.6 convolution_bitcast_fusion
  180.5 5.6 fusion.34
  186.0 4.5 fusion.36
  190.9 1.5 copy-done.7
  192.4 3.5 convert_element_type.40
  195.9 43.2 %reduce-scatter.6.cloned.1.call-done = f32[64,384]{1,0:T(8,128)} async-done(((f32[512,384]{1,0:T(8,128)}), f32[64,384]{1,0:T(8,128)}) %reduce-scatter.6.cloned.1.call-update) | async-done | bytes 98320 | tf_op jit(solution)/shard_map/reduce_scatter | solution.py:206
  239.1 1.7 negate_add_fusion.1
  240.8 64.4 %reduce-scatter.8.cloned.1.call-done = f32[64,384]{1,0:T(8,128)} async-done(((f32[512,384]{1,0:T(8,128)}), f32[64,384]{1,0:T(8,128)}) %reduce-scatter.8.cloned.1.call-update) | async-done | bytes 98320 | tf_op jit(solution)/shard_map/reduce_scatter | solution.py:207
  305.2 1.7 negate_add_fusion
  306.9 220.4 %all-reduce.19.cloned.1.call-done = (f32[3,1024,512]{2,1,0:T(8,128)}, f32[3,1024,512]{2,1,0:T(8,128)}) async-done(((f32[3,1024,512]{2,1,0:T(8,128)}, f32[3,1024,512]{2,1,0:T(8,128)}), (f32[3,1024,512]{2,1,0:T(8,128)}, f32[3,1024,512]{2,1,0:T(8,128)})) %all-reduce.19.cloned.1.call-update) | async-done | bytes 12582928 | tf_op jit(solution)/shard_map/psum | solution.py:161
  527.3 2.3 dynamic-slice_reduce_fusion
  529.7 6.1 multiply_reduce_fusion.2
  536.9 3.9 broadcast_multiply_fusion
  540.8 9.2 %multiply_add_fusion = (f32[3,1024,512]{2,1,0:T(8,128)}, f32[3,1024,512]{2,1,0:T(8,128)}, f32[3,1024,512]{2,1,0:T(8,128)}, f32[3,1024,512]{2,1,0:T(8,128)}) fusion(f32[3,1024,512]{2,1,0:T(8,128)S(1)} %get-tuple-element.100, f32[512]{0:T(512)S(1)} %bitcast.55, f32[512]{0:T(512)S(1)} %bitcast.57, f32[512]{0:T(512)S(1)} %bitcast.53), kind=kLoop, calls=%fused_computation.1 | loop fusion | flops 7864320 | bytes 31463424 | tf_op jit(solution)/shard_map/add | solution.py:43
  550.0 2.9 fusion.17
  553.9 3.6 broadcast_add_fusion
  557.7 6.8 multiply_reduce_fusion.3
  564.5 39.7 %all-reduce.14 = (f32[512]{0:T(512)S(1)}, f32[512]{0:T(512)S(1)}, f32[512]{0:T(512)S(1)}, f32[1536]{0:T(1024)S(1)}, f32[512]{0:T(512)S(1)}, /*index=5*/f32[512]{0:T(512)S(1)}) all-reduce(f32[512]{0:T(512)S(1)} %get-tuple-element.49, f32[512]{0:T(512)S(1)} %get-tuple-element.48, ...), channel_id=3, replica_groups=mesh['dp'=8,'tp'=4] {'dp','tp'}, use_global_device_ids=true, to_apply=%region_15.16.clone | all-reduce | flops 4096 | bytes 32768
  608.0 81.9 %reduce-scatter.10.cloned.1.call-done = f32[16,7]{1,0:T(8,128)} async-done(((f32[512,7]{1,0:T(8,128)}), f32[16,7]{1,0:T(8,128)}) %reduce-scatter.10.cloned.1.call-update) | async-done | bytes 464
  (142 shorter events, 20.2 us)
Async XLA Ops:
  7.2 132.4 %all-gather.4.cloned.1.call-start = ((), (), s32[]{:S(2)}) async-start(), calls=%async_computation.3 | async-start | bytes 3932160 | tf_op jit(solution)/shard_map/all_gather | solution.py:140
  7.9 131.6 %all-gather.6.cloned.1.call-start = ((), (), s32[]{:S(2)}) async-start(), calls=%async_computation.4 | async-start | bytes 3932160 | tf_op jit(solution)/shard_map/all_gather | solution.py:141
  8.7 230.4 %reduce-scatter.6.cloned.1.call-start = ((), (), s32[]{:S(2)}) async-start(), calls=%async_computation.5 | async-start | bytes 884736 | tf_op jit(solution)/shard_map/reduce_scatter | solution.py:206
  9.7 89.1 %collective-permute-start = (bf16[64,384]{1,0:T(8,128)(2,1)S(1)}, bf16[64,384]{1,0:T(8,128)(2,1)S(1)}, u32[]{:S(2)}, u32[]{:S(2)}) collective-permute-start(bf16[64,384]{1,0:T(8,128)(2,1)S(1)} %get-tuple-element.102), channel_id=1, source_target_pairs={{0,28},{4,0},{8,4},{12,8},{16,12},{20,16},{24,20},{28,24},{1,29},{... | collective-permute-start | bytes 147464 | tf_op jit(solution)/shard_map/ppermute | solution.py:25
  98.8 33.9 %collective-permute-start.1 = (bf16[128,384]{1,0:T(8,128)(2,1)S(1)}, bf16[128,384]{1,0:T(8,128)(2,1)S(1)}, u32[]{:S(2)}, u32[]{:S(2)}) collective-permute-start(bf16[128,384]{1,0:T(8,128)(2,1)S(1)} %pad_maximum_fusion.1), channel_id=1, source_target_pairs={{0,24},{4,28},{8,0},{12,4},{16,8},{20,12},{24,16},{28,20},{1,25},{... | collective-permute-start | bytes 294920 | tf_op jit(solution)/shard_map/ppermute | solution.py:25
  132.8 6.6 collective-permute-start.2
  175.4 129.7 %reduce-scatter.8.cloned.1.call-start = ((), (), s32[]{:S(2)}) async-start(), calls=%async_computation.6 | async-start | bytes 884736 | tf_op jit(solution)/shard_map/reduce_scatter | solution.py:207
  180.4 346.9 %all-reduce.19.cloned.1.call-start = ((), (), s32[]{:S(2)}) async-start(), calls=%async_computation.8 | async-start | bytes 25165824 | tf_op jit(solution)/shard_map/psum | solution.py:161
  190.5 499.4 %reduce-scatter.10.cloned.1.call-start = ((), (), s32[]{:S(2)}) async-start(), calls=%async_computation.7 | async-start | bytes 270336
  192.4 46.7 %copy-start.12 = (f32[64,384]{1,0:T(8,128)S(1)}, f32[64,384]{1,0:T(8,128)}, u32[]{:S(2)}) copy-start(f32[64,384]{1,0:T(8,128)} %param.55) | copy-start | bytes 294916
  192.4 112.8 %copy-start.9 = (f32[64,384]{1,0:T(8,128)S(1)}, f32[64,384]{1,0:T(8,128)}, u32[]{:S(2)}) copy-start(f32[64,384]{1,0:T(8,128)} %param.39) | copy-start | bytes 294916
  557.4 46.8 %copy-start.17 = (f32[16]{0:T(128)S(1)}, f32[16]{0:T(128)}, u32[]{:S(2)}) copy-start(f32[16]{0:T(128)} %param.34) | copy-start | bytes 196
  557.4 46.8 %copy-start.18 = (f32[16]{0:T(128)S(1)}, f32[16]{0:T(128)}, u32[]{:S(2)}) copy-start(f32[16]{0:T(128)} %param.52) | copy-start | bytes 196
  557.5 46.8 %copy-start.19 = (f32[16]{0:T(128)S(1)}, f32[16]{0:T(128)}, u32[]{:S(2)}) copy-start(f32[16]{0:T(128)} %param.43) | copy-start | bytes 196
  557.5 47.4 %copy-start.20 = (f32[16]{0:T(128)S(1)}, f32[16]{0:T(128)}, u32[]{:S(2)}) copy-start(f32[16]{0:T(128)} %param.35) | copy-start | bytes 196
  557.5 47.4 %copy-start.21 = (f32[16]{0:T(128)S(1)}, f32[16]{0:T(128)}, u32[]{:S(2)}) copy-start(f32[16]{0:T(128)} %param.53) | copy-start | bytes 196
  557.5 47.4 %copy-start.22 = (f32[16]{0:T(128)S(1)}, f32[16]{0:T(128)}, u32[]{:S(2)}) copy-start(f32[16]{0:T(128)} %param.44) | copy-start | bytes 196
  557.5 48.0 %copy-start.23 = (f32[16]{0:T(128)S(1)}, f32[16]{0:T(128)}, u32[]{:S(2)}) copy-start(f32[16]{0:T(128)} %param.36) | copy-start | bytes 196
  557.5 48.0 %copy-start.24 = (f32[16]{0:T(128)S(1)}, f32[16]{0:T(128)}, u32[]{:S(2)}) copy-start(f32[16]{0:T(128)} %param.54) | copy-start | bytes 196
  557.5 47.9 %copy-start.25 = (f32[16]{0:T(128)S(1)}, f32[16]{0:T(128)}, u32[]{:S(2)}) copy-start(f32[16]{0:T(128)} %param.45) | copy-start | bytes 196
  557.5 48.6 %copy-start.26 = (f32[16]{0:T(128)S(1)}, f32[16]{0:T(128)}, u32[]{:S(2)}) copy-start(f32[16]{0:T(128)} %param.40) | copy-start | bytes 196
  557.6 48.5 %copy-start.27 = (f32[16]{0:T(128)S(1)}, f32[16]{0:T(128)}, u32[]{:S(2)}) copy-start(f32[16]{0:T(128)} %param.58) | copy-start | bytes 196
  557.6 48.5 %copy-start.28 = (f32[16]{0:T(128)S(1)}, f32[16]{0:T(128)}, u32[]{:S(2)}) copy-start(f32[16]{0:T(128)} %param.49) | copy-start | bytes 196
  557.6 49.1 %copy-start.29 = (f32[16]{0:T(128)S(1)}, f32[16]{0:T(128)}, u32[]{:S(2)}) copy-start(f32[16]{0:T(128)} %param.41) | copy-start | bytes 196
  557.6 49.1 %copy-start.30 = (f32[16]{0:T(128)S(1)}, f32[16]{0:T(128)}, u32[]{:S(2)}) copy-start(f32[16]{0:T(128)} %param.59) | copy-start | bytes 196
  557.6 49.1 %copy-start.31 = (f32[16]{0:T(128)S(1)}, f32[16]{0:T(128)}, u32[]{:S(2)}) copy-start(f32[16]{0:T(128)} %param.50) | copy-start | bytes 196
  557.6 49.7 %copy-start.32 = (f32[48]{0:T(128)S(1)}, f32[48]{0:T(128)}, u32[]{:S(2)}) copy-start(f32[48]{0:T(128)} %param.38) | copy-start | bytes 580
  557.6 49.7 %copy-start.33 = (f32[48]{0:T(128)S(1)}, f32[48]{0:T(128)}, u32[]{:S(2)}) copy-start(f32[48]{0:T(128)} %param.56) | copy-start | bytes 580
  557.6 49.7 %copy-start.34 = (f32[48]{0:T(128)S(1)}, f32[48]{0:T(128)}, u32[]{:S(2)}) copy-start(f32[48]{0:T(128)} %param.47) | copy-start | bytes 580
  557.7 133.0 %copy-start.13 = (f32[16,7]{0,1:T(8,128)S(1)}, f32[16,7]{0,1:T(8,128)}, u32[]{:S(2)}) copy-start(f32[16,7]{0,1:T(8,128)} %param.33) | copy-start | bytes 1348
  557.7 133.0 %copy-start.15 = (f32[16,7]{0,1:T(8,128)S(1)}, f32[16,7]{0,1:T(8,128)}, u32[]{:S(2)}) copy-start(f32[16,7]{0,1:T(8,128)} %param.51) | copy-start | bytes 1348
  557.7 133.0 %copy-start.16 = (f32[16,7]{0,1:T(8,128)S(1)}, f32[16,7]{0,1:T(8,128)}, u32[]{:S(2)}) copy-start(f32[16,7]{0,1:T(8,128)} %param.42) | copy-start | bytes 1348
  (16 other events, 165.8 us)
Sparse Core Ops, SparseCore 0:
  9.6 31.9 all-gather.3
  43.1 29.0 all-gather.5
  175.6 63.5 reduce-scatter.5
  242.8 62.2 reduce-scatter.7
  307.6 219.6 all-reduce.18
  554.0 135.8 reduce-scatter.9
